TPU v7x, 32 devices: a whole 2x2x4 slice. The times are simulated.
32 devices in a mesh: col: 4 (over y, x), dev: 4 (over z), ao: 2 (over core).
Axes of the slice: x: 2, y: 2, z: 4, core: 2. Of those that a mesh axis runs over, the one named last changes fastest.
Arguments:
- raw_ints: bfloat16 [1024, 32, 512], P('dev', None, 'col'), may hold values from -1.078125 to 1.078125
- metric: bfloat16 [1024, 1024], P('dev'), may hold values from -0.1875 to 0.1875
- amplitudes: bfloat16 [512, 512, 2048], P('col', 'dev', 'ao'), may hold values from -0.017944336 to 0.017944336
- pair_list: int32 [2, 2048], P(None, 'ao'), may hold values from 0 to 63
- occ_energy: float32 [64], replicated, may hold values from -2 to -0.3
- vir_energy: float32 [512], replicated, may hold values from 0.2 to 3
- window_ids: int32 [32], replicated, may hold values from 0 to 511, as said below
Outputs:
- residual: float32 [1024, 2048], P(('col', 'dev'), 'ao')
Inputs may be any that keep to these rules, and one draw needn't show every extreme that they name: `window_ids`: distinct virtual orbitals; 0 and 511 are always among them.
All inputs are finite; a program needn't handle non-finite values.
Results may differ from a plain program's by a relative error of at most 0.0041.
Values may be sent and summed in bfloat16 or wider, within the bound.
No kernel may reach another device: no remote copies, remote signals or barrier semaphores. Data moves between devices by JAX's collectives and lax.ppermute only.
A program may use at most 192 MiB of HBM per device.

v0:
```python
import jax
import jax.numpy as jnp
from jax import lax
from jax.sharding import PartitionSpec as P


def select_energy(positions, table):
    labels = jnp.arange(table.shape[0], dtype=jnp.int32)
    return jnp.sum(jnp.where(positions[:, None] == labels[None, :], table[None, :], 0.0), axis=1)


def on_device(raw_ints, metric, amplitudes, pair_list, occ_energy, vir_energy, window_ids):
    full_width = raw_ints.shape[1]
    portion = full_width // lax.axis_size("ao")
    own_rows = lax.dynamic_slice_in_dim(raw_ints, lax.axis_index("ao") * portion, portion, 1)
    local_aux = metric.shape[0]
    rows_used = own_rows.shape[1]
    c_block = own_rows.shape[2]
    raw_block = lax.all_gather(own_rows, "dev", axis=0, tiled=True)
    row_count = raw_block.shape[0]
    transformed = jnp.dot(
        metric,
        raw_block.reshape(row_count, rows_used * c_block),
        preferred_element_type=jnp.float32,
    )
    transformed = transformed.astype(jnp.bfloat16).reshape(local_aux, rows_used, c_block)
    spread = lax.all_gather(transformed, "col", axis=2, tiled=True)
    right_factor = lax.all_to_all(spread, "dev", split_axis=2, concat_axis=0, tiled=True)
    d_block = right_factor.shape[2]
    contract = (((0,), (0,)), ((), ()))
    left_factor = lax.all_gather(transformed, "dev", axis=0, tiled=True)
    right_factor = lax.all_gather(right_factor, "ao", axis=1, tiled=True)
    all_aux = left_factor.shape[0]
    own_ladder = lax.dot_general(
        left_factor.reshape(all_aux, rows_used * c_block),
        right_factor.reshape(all_aux, full_width * d_block),
        contract,
        preferred_element_type=jnp.float32,
    )
    ladder_flat = lax.all_gather(own_ladder.astype(jnp.bfloat16), "ao", axis=0, tiled=True)
    ladder = ladder_flat.reshape(full_width, c_block, full_width, d_block)
    ladder = jnp.transpose(ladder, (0, 2, 1, 3)).reshape(full_width * full_width, c_block * d_block)
    partial_value = jnp.dot(
        ladder,
        amplitudes.reshape(c_block * d_block, amplitudes.shape[2]),
        preferred_element_type=jnp.float32,
    )
    summed = lax.psum_scatter(partial_value, ("col", "dev"), scatter_dimension=0, tiled=True)
    row_total = summed.shape[0]
    global_rows = lax.axis_index(("col", "dev")) * row_total + jnp.arange(
        row_total, dtype=jnp.int32
    )
    window_energy = select_energy(window_ids, vir_energy)
    energy_first = select_energy(global_rows // full_width, window_energy)
    energy_second = select_energy(global_rows % full_width, window_energy)
    energy_i = select_energy(pair_list[0], occ_energy)
    energy_j = select_energy(pair_list[1], occ_energy)
    denominator = (energy_i + energy_j)[None, :] - (energy_first + energy_second)[:, None]
    return summed / denominator


def solution(mesh):
    in_specs = (
        P("dev", None, "col"),
        P("dev", None),
        P("col", "dev", "ao"),
        P(None, "ao"),
        P(),
        P(),
        P(),
    )
    out_specs = P(("col", "dev"), "ao")
    return jax.shard_map(
        on_device, mesh=mesh, in_specs=in_specs, out_specs=out_specs, check_vma=False
    )
```

profile of v0, /device:TPU:0, one launch (start us, length us, event | category | flops | bytes accessed | tf_op | source)
XLA Modules:
  0.0 614.5 jit_solution(7813897264550243271)
XLA Ops:
  6.5 0.0 copy-start
  6.5 0.0 all-gather.6.cloned.1.call-start
  6.5 1.6 copy-done
  8.1 1.1 constant_dynamic-slice_fusion
  9.3 0.0 all-gather.6.cloned.1.call-update
  9.3 0.0 all-gather.10.cloned.1.call-start
  9.3 83.6 %all-gather.6.cloned.1.call-done = bf16[1024,16,128]{2,1,0:T(8,128)(2,1)} async-done(((bf16[256,16,128]{2,1,0:T(8,128)(2,1)}), bf16[1024,16,128]{2,1,0:T(8,128)(2,1)}) %all-gather.6.cloned.1.call-update) | async-done | bytes 4194320 | tf_op jit(solution)/shard_map/all_gather | solution.py:19
  92.9 4.5 fusion.8
  97.4 0.0 copy-start.2
  97.4 1.6 copy.19
  98.9 0.0 all-gather.10.cloned.1.call-update
  99.0 51.2 %all-gather.10.cloned.1.call-done = bf16[256,16,512]{0,1,2:T(8,128)(2,1)} async-done(((bf16[256,16,128]{0,1,2:T(8,128)(2,1)}), bf16[256,16,512]{0,1,2:T(8,128)(2,1)}) %all-gather.10.cloned.1.call-update) | async-done | bytes 4194320 | tf_op jit(solution)/shard_map/all_gather | solution.py:27
  150.2 4.8 all-to-all-start
  155.0 0.0 all-gather.8.cloned.1.call-start
  155.1 0.0 copy-done.2
  155.1 0.7 all-gather.8.cloned.1.call-update
  155.8 0.0 all-gather.12.cloned.1.call-start
  155.8 159.9 %all-to-all-done = bf16[256,16,512]{0,1,2:T(8,128)(2,1)} async-done(((bf16[256,16,512]{0,1,2:T(8,128)(2,1)}), bf16[256,16,512]{0,1,2:T(8,128)(2,1)}, u32[]{:S(2)}, u32[]{:S(2)}) %all-to-all-start) | async-done | bytes 4194336 | tf_op jit(solution)/shard_map/all_to_all | solution.py:28
  315.8 9.0 %copy.21 = bf16[4,256,16,128]{3,2,1,0:T(8,128)(2,1)} copy(bf16[4,256,16,128]{1,2,3,0:T(8,128)(2,1)} %bitcast.6) | data formatting | bytes 8388608 | tf_op jit(solution)/shard_map/all_to_all | solution.py:28
  324.7 0.0 all-gather.12.cloned.1.call-update
  324.7 0.0 all-gather.14.cloned.1.call-start
  324.8 0.0 all-gather.8.cloned.1.call-done
  324.8 16.3 %all-gather.12.cloned.1.call-done = bf16[1024,32,128]{2,1,0:T(8,128)(2,1)} async-done(((bf16[1024,16,128]{2,1,0:T(8,128)(2,1)}), bf16[1024,32,128]{2,1,0:T(8,128)(2,1)}) %all-gather.12.cloned.1.call-update) | async-done | bytes 8388624 | tf_op jit(solution)/shard_map/all_gather | solution.py:32
  341.1 24.3 %convolution_convert_fusion = bf16[2048,4096]{1,0:T(8,128)(2,1)} fusion(bf16[1024,2048]{0,1:T(8,128)(2,1)} %bitcast.43, bf16[128,8,32,128]{3,2,1,0:T(8,128)(2,1)} %bitcast.42), kind=kOutput, calls=%fused_computation.3 | convolution fusion | flops 17188257792 | bytes 29360128 | tf_op jit(solution)/shard_map/dot_general | solution.py:34
  365.5 0.0 all-gather.14.cloned.1.call-update
  365.5 0.2 reduce-scatter.2.cloned.1.call-start
  365.7 52.1 %all-gather.14.cloned.1.call-done = bf16[4096,4096]{1,0:T(8,128)(2,1)} async-done(((bf16[2048,4096]{1,0:T(8,128)(2,1)}), bf16[4096,4096]{1,0:T(8,128)(2,1)}) %all-gather.14.cloned.1.call-update) | async-done | bytes 33554448 | tf_op jit(solution)/shard_map/all_gather | solution.py:40
  417.9 23.1 %copy.26 = bf16[512,8,32,128]{3,2,1,0:T(8,128)(2,1)} copy(bf16[512,8,32,128]{3,1,2,0:T(8,128)(2,1)} %bitcast.34) | data formatting | bytes 67108864
  440.9 23.0 %copy.22 = bf16[32,128,32,128]{3,1,2,0:T(8,128)(2,1)} copy(bf16[32,128,32,128]{3,2,1,0:T(8,128)(2,1)} %bitcast.33) | data formatting | bytes 67108864 | tf_op jit(solution)/shard_map/reshape | solution.py:41
  464.0 0.0 copy-start.4
  464.0 0.0 copy-start.6
  464.0 0.0 copy-start.3
  464.0 0.0 copy-start.5
  464.0 0.0 copy-start.1
  464.0 43.1 %fusion = f32[1024,1024]{1,0:T(8,128)} fusion(bf16[16384,1024]{1,0:T(8,128)(2,1)} %bitcast.41, bf16[128,8,128,128]{3,2,1,0:T(8,128)(2,1)} %bitcast.35), kind=kOutput, calls=%fused_computation | convolution fusion | flops 34359738368 | bytes 71303168 | tf_op jit(solution)/shard_map/dot_general | solution.py:43
  507.1 0.0 reduce-scatter.2.cloned.1.call-update
  507.1 0.0 copy-done.4
  507.2 0.0 copy-done.6
  507.2 0.2 select_reduce_fusion.2
  507.4 0.1 select_reduce_fusion.3
  507.5 0.0 copy-done.3
  507.5 0.0 copy-done.5
  507.5 0.2 select_reduce_fusion
  507.7 98.2 %reduce-scatter.2.cloned.1.call-done = f32[64,1024]{1,0:T(8,128)} async-done(((f32[1024,1024]{1,0:T(8,128)}), f32[64,1024]{1,0:T(8,128)}) %reduce-scatter.2.cloned.1.call-update) | async-done | bytes 262160 | tf_op jit(solution)/shard_map/reduce_scatter | solution.py:48
  605.8 1.8 subtract_divide_fusion
  607.6 0.0 copy-done.1
  (4 shorter events, 0.0 us)
Async XLA Ops:
  6.5 1.6 copy-start
  6.5 86.4 %all-gather.6.cloned.1.call-start = ((), (), s32[]{:S(2)}) async-start(), calls=%async_computation.2 | async-start | bytes 5242880 | tf_op jit(solution)/shard_map/all_gather | solution.py:19
  9.3 140.9 %all-gather.10.cloned.1.call-start = ((), (), s32[]{:S(2)}) async-start(), calls=%async_computation.4 | async-start | bytes 5242880 | tf_op jit(solution)/shard_map/all_gather | solution.py:27
  97.4 57.7 %copy-start.2 = (bf16[2048,256]{1,0:T(8,128)(2,1)}, bf16[2048,256]{1,0:T(8,128)(2,1)S(1)}, u32[]{:S(2)}) copy-start(bf16[2048,256]{1,0:T(8,128)(2,1)S(1)} %fusion.8) | copy-start | bytes 3145732
  150.2 165.6 %all-to-all-start = ((bf16[256,16,512]{0,1,2:T(8,128)(2,1)}), bf16[256,16,512]{0,1,2:T(8,128)(2,1)}, u32[]{:S(2)}, u32[]{:S(2)}) async-start(bf16[256,16,512]{0,1,2:T(8,128)(2,1)} %all-gather.10.cloned.1.call-done), calls=%async_computation | async-start | bytes 8388608 | tf_op jit(solution)/shard_map/all_to_all | solution.py:28
  155.0 169.8 %all-gather.8.cloned.1.call-start = ((), (), s32[]{:S(2)}) async-start(), calls=%async_computation.3 | async-start | bytes 5242880 | tf_op jit(solution)/shard_map/all_gather | solution.py:31
  155.8 185.3 %all-gather.12.cloned.1.call-start = ((), (), s32[]{:S(2)}) async-start(), calls=%async_computation.5 | async-start | bytes 12582912 | tf_op jit(solution)/shard_map/all_gather | solution.py:32
  324.7 93.1 %all-gather.14.cloned.1.call-start = ((), (), s32[]{:S(2)}) async-start(), calls=%async_computation.6 | async-start | bytes 50331648 | tf_op jit(solution)/shard_map/all_gather | solution.py:40
  365.5 240.4 %reduce-scatter.2.cloned.1.call-start = ((), (), s32[]{:S(2)}) async-start(), calls=%async_computation.7 | async-start | bytes 4456448 | tf_op jit(solution)/shard_map/reduce_scatter | solution.py:48
  464.0 43.2 %copy-start.4 = (f32[512]{0:T(512)S(1)}, f32[512]{0:T(512)}, u32[]{:S(2)}) copy-start(f32[512]{0:T(512)} %param.12) | copy-start | bytes 6148
  464.0 43.2 %copy-start.6 = (s32[32]{0:T(128)S(1)}, s32[32]{0:T(128)}, u32[]{:S(2)}) copy-start(s32[32]{0:T(128)} %param.13) | copy-start | bytes 388
  464.0 43.5 %copy-start.3 = (s32[2,1024]{1,0:T(2,128)S(1)}, s32[2,1024]{1,0:T(2,128)}, u32[]{:S(2)}) copy-start(s32[2,1024]{1,0:T(2,128)} %param.10) | copy-start | bytes 24580
  464.0 43.5 %copy-start.5 = (f32[64]{0:T(128)S(1)}, f32[64]{0:T(128)}, u32[]{:S(2)}) copy-start(f32[64]{0:T(128)} %param.11) | copy-start | bytes 772
  464.0 143.6 %copy-start.1 = (bf16[256,32,128]{2,1,0:T(8,128)(2,1)S(1)}, bf16[256,32,128]{2,1,0:T(8,128)(2,1)}, u32[]{:S(2)}) copy-start(bf16[256,32,128]{2,1,0:T(8,128)(2,1)} %param.7) | copy-start | bytes 6291460
Sparse Core Ops, SparseCore 0:
  9.4 83.4 all-gather.5
  99.1 51.0 all-gather.9
  157.4 150.1 all-gather.7
  324.9 16.1 all-gather.11
  365.6 52.2 all-gather.13
  507.2 98.5 reduce-scatter.1
where the time goes:
time: 615 us; the launch traced here: 614 us
  waiting for transfers between devices  462 us (75%)
  matrix products  71.9 us (12%)
  local copies, waits for them, and re-layouts  59.4 us (10%)
  between operations  13.6 us (2%)
    all_to_all x1, waiting for transfers between devices, on_device(): lax.all_to_all(spread, 'dev', split_axis=2, concat_axis=0, tiled=True)  160 us
    reduce_scatter x1, waiting for transfers between devices, on_device(): lax.psum_scatter(partial_value, ('col', 'dev'), scatter_dimension=0, tile...  98.2 us
    all_gather x1, waiting for transfers between devices, on_device(): raw_block = lax.all_gather(own_rows, 'dev', axis=0, tiled=True)  83.6 us
    all_gather x1, waiting for transfers between devices, on_device(): lax.all_gather(own_ladder.astype(jnp.bfloat16), 'ao', axis=0, tiled=True)  52.1 us
    all_gather x1, waiting for transfers between devices, on_device(): spread = lax.all_gather(transformed, 'col', axis=2, tiled=True)  51.2 us
    dot_general x1, matrix products, on_device(): jnp.dot(ladder, amplitudes.reshape(c_block * d_block, amplitudes.shape[2]...  43.1 us
    unnamed x15, local copies, waits for them, and re-layouts  24.7 us
    dot_general x1, matrix products, on_device(): lax.dot_general(left_factor.reshape(all_aux, rows_used * c_block), right_...  24.3 us
  transfers between devices with their start and end apart: 7, of which 6 were waited for; matrix products, arithmetic and copies ran while one was open for 2% of the time, Pallas kernels for 0%

commit v1 on v0

--- a/solution.py
+++ b/solution.py
@@ -24,7 +24,25 @@
         preferred_element_type=jnp.float32,
     )
     transformed = transformed.astype(jnp.bfloat16).reshape(local_aux, rows_used, c_block)
-    spread = lax.all_gather(transformed, "col", axis=2, tiled=True)
+    count, index, rows = (lax.axis_size("col"), lax.axis_index("col"), transformed.shape[2])
+    upward = [(i, (i + 1) % count) for i in range(count)]
+    left = [(i, (i - 1) % count) for i in range(count)]
+    spread = jnp.zeros(
+        (*transformed.shape[:2], count * rows, *transformed.shape[2 + 1 :]), transformed.dtype
+    )
+    spread = lax.dynamic_update_slice_in_dim(spread, transformed, index * rows, axis=2)
+    from_left = from_right = transformed
+    half = count // 2
+    for step in range(1, half + 1):
+        from_left = lax.ppermute(from_left, "col", upward)
+        spread = lax.dynamic_update_slice_in_dim(
+            spread, from_left, (index - step) % count * rows, axis=2
+        )
+        if step < count - half:
+            from_right = lax.ppermute(from_right, "col", left)
+            spread = lax.dynamic_update_slice_in_dim(
+                spread, from_right, (index + step) % count * rows, axis=2
+            )
     right_factor = lax.all_to_all(spread, "dev", split_axis=2, concat_axis=0, tiled=True)
     d_block = right_factor.shape[2]
     contract = (((0,), (0,)), ((), ()))

time: 615 us -> 637 us (1.036)
  waiting for transfers between devices: 462 us -> 473 us
  local copies, waits for them, and re-layouts: 59.4 us -> 67.1 us
    ppermute x0 -> x3, waiting for transfers between devices: none -> 63.9 us  [the longest x2 42.9 us: on_device(): from_left = lax.ppermute(from_left, 'col', upward)]
    all_gather x1 -> x0, waiting for transfers between devices: 51.2 us -> none  [on_device(): spread = lax.all_gather(transformed, 'col', axis=2, tiled=True)]
  transfers between devices with their start and end apart: 7 -> 9, of which waited for: 6 -> 8; matrix products, arithmetic and copies ran while one was open for 2% -> 2% of each run, Pallas kernels for 0% -> 0%
where the time goes in v1:
time: 637 us
  waiting for transfers between devices  473 us (74%)
  matrix products  71.9 us (11%)
  local copies, waits for them, and re-layouts  67.1 us (11%)
  between operations  13.3 us (2%)
  starting transfers between devices  8.77 us (1%)
    all_to_all x1, waiting for transfers between devices, on_device(): lax.all_to_all(spread, 'dev', split_axis=2, concat_axis=0, tiled=True)  159 us
    reduce_scatter x1, waiting for transfers between devices, on_device(): lax.psum_scatter(partial_value, ('col', 'dev'), scatter_dimension=0, tile...  97.6 us
    all_gather x1, waiting for transfers between devices, on_device(): raw_block = lax.all_gather(own_rows, 'dev', axis=0, tiled=True)  83.6 us
    all_gather x1, waiting for transfers between devices, on_device(): lax.all_gather(own_ladder.astype(jnp.bfloat16), 'ao', axis=0, tiled=True)  52.2 us
    dot_general x1, matrix products, on_device(): jnp.dot(ladder, amplitudes.reshape(c_block * d_block, amplitudes.shape[2]...  43.1 us
    ppermute x2, waiting for transfers between devices, on_device(): from_left = lax.ppermute(from_left, 'col', upward)  42.9 us
    unnamed x15, local copies, waits for them, and re-layouts  25.3 us
    dot_general x1, matrix products, on_device(): lax.dot_general(left_factor.reshape(all_aux, rows_used * c_block), right_...  24.3 us
  transfers between devices with their start and end apart: 9, of which 8 were waited for; matrix products, arithmetic and copies ran while one was open for 2% of the time, Pallas kernels for 0%

profile of v1, /device:TPU:0, one launch (start us, length us, event | category | flops | bytes accessed | tf_op | source)
XLA Modules:
  0.0 636.7 jit_solution(5414142721861886599)
XLA Ops:
  6.5 0.0 copy-start
  6.5 0.0 all-gather.5.cloned.1.call-start
  6.5 1.6 copy-done
  8.1 1.2 constant_dynamic-slice_fusion
  9.3 0.0 all-gather.5.cloned.1.call-update
  9.3 83.6 %all-gather.5.cloned.1.call-done = bf16[1024,16,128]{2,1,0:T(8,128)(2,1)} async-done(((bf16[256,16,128]{2,1,0:T(8,128)(2,1)}), bf16[1024,16,128]{2,1,0:T(8,128)(2,1)}) %all-gather.5.cloned.1.call-update) | async-done | bytes 4194320 | tf_op jit(solution)/shard_map/all_gather | solution.py:19
  92.9 4.5 fusion.8
  97.4 0.0 copy-start.2
  97.4 2.3 broadcast_in_dim.62
  99.7 1.9 fusion.11
  101.6 1.5 collective-permute-start
  103.2 1.4 collective-permute-start.1
  104.5 24.2 %collective-permute-done = bf16[256,16,128]{0,1,2:T(8,128)(2,1)S(1)} collective-permute-done((bf16[256,16,128]{0,1,2:T(8,128)(2,1)}, bf16[256,16,128]{0,1,2:T(8,128)(2,1)S(1)}, u32[]{:S(2)}, u32[]{:S(2)}) %collective-permute-start) | collective-permute-done | bytes 1048608 | tf_op jit(solution)/shard_map/ppermute | solution.py:37
  128.8 0.6 collective-permute-start.2
  129.4 1.1 constant_dynamic-update-slice_fusion.2
  130.5 0.0 copy-done.2
  130.5 20.9 %collective-permute-done.1 = bf16[256,16,128]{0,1,2:T(8,128)(2,1)} collective-permute-done((bf16[256,16,128]{0,1,2:T(8,128)(2,1)}, bf16[256,16,128]{0,1,2:T(8,128)(2,1)}, u32[]{:S(2)}, u32[]{:S(2)}) %collective-permute-start.1) | collective-permute-done | bytes 1048608 | tf_op jit(solution)/shard_map/ppermute | solution.py:42
  151.4 2.3 constant_dynamic-update-slice_fusion.1
  153.7 18.7 %collective-permute-done.2 = bf16[256,16,128]{0,1,2:T(8,128)(2,1)S(1)} collective-permute-done((bf16[256,16,128]{0,1,2:T(8,128)(2,1)S(1)}, bf16[256,16,128]{0,1,2:T(8,128)(2,1)S(1)}, u32[]{:S(2)}, u32[]{:S(2)}) %collective-permute-start.2) | collective-permute-done | bytes 1048608 | tf_op jit(solution)/shard_map/ppermute | solution.py:37
  172.4 1.1 constant_dynamic-update-slice_fusion
  173.5 4.8 all-to-all-start
  178.4 0.0 all-gather.7.cloned.1.call-start
  178.4 0.7 all-gather.7.cloned.1.call-update
  179.1 0.0 all-gather.9.cloned.1.call-start
  179.2 159.1 %all-to-all-done = bf16[256,16,512]{0,1,2:T(8,128)(2,1)} async-done(((bf16[256,16,512]{0,1,2:T(8,128)(2,1)}), bf16[256,16,512]{0,1,2:T(8,128)(2,1)}, u32[]{:S(2)}, u32[]{:S(2)}) %all-to-all-start) | async-done | bytes 4194336 | tf_op jit(solution)/shard_map/all_to_all | solution.py:46
  338.3 9.0 %copy.21 = bf16[4,256,16,128]{3,2,1,0:T(8,128)(2,1)} copy(bf16[4,256,16,128]{1,2,3,0:T(8,128)(2,1)} %bitcast.6) | data formatting | bytes 8388608 | tf_op jit(solution)/shard_map/all_to_all | solution.py:46
  347.2 0.0 all-gather.9.cloned.1.call-update
  347.2 0.0 all-gather.11.cloned.1.call-start
  347.3 0.0 all-gather.7.cloned.1.call-done
  347.3 16.3 %all-gather.9.cloned.1.call-done = bf16[1024,32,128]{2,1,0:T(8,128)(2,1)} async-done(((bf16[1024,16,128]{2,1,0:T(8,128)(2,1)}), bf16[1024,32,128]{2,1,0:T(8,128)(2,1)}) %all-gather.9.cloned.1.call-update) | async-done | bytes 8388624 | tf_op jit(solution)/shard_map/all_gather | solution.py:50
  363.6 24.3 %convolution_convert_fusion = bf16[2048,4096]{1,0:T(8,128)(2,1)} fusion(bf16[1024,2048]{0,1:T(8,128)(2,1)} %bitcast.43, bf16[128,8,32,128]{3,2,1,0:T(8,128)(2,1)} %bitcast.42), kind=kOutput, calls=%fused_computation.3 | convolution fusion | flops 17188257792 | bytes 29360128 | tf_op jit(solution)/shard_map/dot_general | solution.py:52
  388.0 0.0 all-gather.11.cloned.1.call-update
  388.0 0.2 reduce-scatter.2.cloned.1.call-start
  388.2 52.2 %all-gather.11.cloned.1.call-done = bf16[4096,4096]{1,0:T(8,128)(2,1)} async-done(((bf16[2048,4096]{1,0:T(8,128)(2,1)}), bf16[4096,4096]{1,0:T(8,128)(2,1)}) %all-gather.11.cloned.1.call-update) | async-done | bytes 33554448 | tf_op jit(solution)/shard_map/all_gather | solution.py:58
  440.4 23.1 %copy.26 = bf16[512,8,32,128]{3,2,1,0:T(8,128)(2,1)} copy(bf16[512,8,32,128]{3,1,2,0:T(8,128)(2,1)} %bitcast.34) | data formatting | bytes 67108864
  463.4 23.1 %copy.22 = bf16[32,128,32,128]{3,1,2,0:T(8,128)(2,1)} copy(bf16[32,128,32,128]{3,2,1,0:T(8,128)(2,1)} %bitcast.33) | data formatting | bytes 67108864 | tf_op jit(solution)/shard_map/reshape | solution.py:59
  486.5 0.0 copy-start.1
  486.5 43.1 %fusion = f32[1024,1024]{1,0:T(8,128)} fusion(bf16[16384,1024]{1,0:T(8,128)(2,1)} %bitcast.41, bf16[128,8,128,128]{3,2,1,0:T(8,128)(2,1)} %bitcast.35), kind=kOutput, calls=%fused_computation | convolution fusion | flops 34359738368 | bytes 71303168 | tf_op jit(solution)/shard_map/dot_general | solution.py:61
  529.6 0.0 copy-start.4
  529.6 0.0 copy-start.6
  529.6 0.0 copy-start.3
  529.6 0.0 copy-start.5
  529.6 0.0 reduce-scatter.2.cloned.1.call-update
  529.7 0.6 copy-done.4
  530.3 0.0 copy-done.6
  530.3 0.2 select_reduce_fusion.2
  530.4 0.1 select_reduce_fusion.3
  530.5 0.0 copy-done.3
  530.6 0.0 copy-done.5
  530.6 0.2 select_reduce_fusion
  530.8 97.6 %reduce-scatter.2.cloned.1.call-done = f32[64,1024]{1,0:T(8,128)} async-done(((f32[1024,1024]{1,0:T(8,128)}), f32[64,1024]{1,0:T(8,128)}) %reduce-scatter.2.cloned.1.call-update) | async-done | bytes 262160 | tf_op jit(solution)/shard_map/reduce_scatter | solution.py:66
  628.4 1.8 subtract_divide_fusion
  630.2 0.0 copy-done.1
  (4 shorter events, 0.0 us)
Async XLA Ops:
  6.5 1.6 copy-start
  6.5 86.4 %all-gather.5.cloned.1.call-start = ((), (), s32[]{:S(2)}) async-start(), calls=%async_computation.2 | async-start | bytes 5242880 | tf_op jit(solution)/shard_map/all_gather | solution.py:19
  97.4 33.1 %copy-start.2 = (bf16[2048,256]{1,0:T(8,128)(2,1)}, bf16[2048,256]{1,0:T(8,128)(2,1)S(1)}, u32[]{:S(2)}) copy-start(bf16[2048,256]{1,0:T(8,128)(2,1)S(1)} %fusion.8) | copy-start | bytes 3145732
  101.6 27.1 %collective-permute-start = (bf16[256,16,128]{0,1,2:T(8,128)(2,1)}, bf16[256,16,128]{0,1,2:T(8,128)(2,1)S(1)}, u32[]{:S(2)}, u32[]{:S(2)}) collective-permute-start(bf16[256,16,128]{0,1,2:T(8,128)(2,1)} %get-tuple-element.9), channel_id=1, source_target_pairs={{0,8},{8,16},{16,24},{24,0},{1,9},{9,17},{17,25},{25,1},{2,10},{10... | collective-permute-start | bytes 3145736 | tf_op jit(solution)/shard_map/ppermute | solution.py:37
  103.2 48.2 %collective-permute-start.1 = (bf16[256,16,128]{0,1,2:T(8,128)(2,1)}, bf16[256,16,128]{0,1,2:T(8,128)(2,1)}, u32[]{:S(2)}, u32[]{:S(2)}) collective-permute-start(bf16[256,16,128]{0,1,2:T(8,128)(2,1)} %get-tuple-element.9), channel_id=1, source_target_pairs={{0,24},{8,0},{16,8},{24,16},{1,25},{9,1},{17,9},{25,17},{2,26},{10... | collective-permute-start | bytes 3145736 | tf_op jit(solution)/shard_map/ppermute | solution.py:42
  128.8 43.7 %collective-permute-start.2 = (bf16[256,16,128]{0,1,2:T(8,128)(2,1)S(1)}, bf16[256,16,128]{0,1,2:T(8,128)(2,1)S(1)}, u32[]{:S(2)}, u32[]{:S(2)}) collective-permute-start(bf16[256,16,128]{0,1,2:T(8,128)(2,1)S(1)} %collective-permute-done), channel_id=1, source_target_pairs={{0,8},{8,16},{16,24},{24,0},{1,9},{9,17},{17,25},{25,1},{2,10},{10... | collective-permute-start | bytes 3145736 | tf_op jit(solution)/shard_map/ppermute | solution.py:37
  173.5 164.8 %all-to-all-start = ((bf16[256,16,512]{0,1,2:T(8,128)(2,1)}), bf16[256,16,512]{0,1,2:T(8,128)(2,1)}, u32[]{:S(2)}, u32[]{:S(2)}) async-start(bf16[256,16,512]{0,1,2:T(8,128)(2,1)} %constant_dynamic-update-slice_fusion), calls=%async_computation | async-start | bytes 8388608 | tf_op jit(solution)/shard_map/all_to_all | solution.py:46
  178.4 168.9 %all-gather.7.cloned.1.call-start = ((), (), s32[]{:S(2)}) async-start(), calls=%async_computation.3 | async-start | bytes 5242880 | tf_op jit(solution)/shard_map/all_gather | solution.py:49
  179.1 184.5 %all-gather.9.cloned.1.call-start = ((), (), s32[]{:S(2)}) async-start(), calls=%async_computation.4 | async-start | bytes 12582912 | tf_op jit(solution)/shard_map/all_gather | solution.py:50
  347.2 93.1 %all-gather.11.cloned.1.call-start = ((), (), s32[]{:S(2)}) async-start(), calls=%async_computation.5 | async-start | bytes 50331648 | tf_op jit(solution)/shard_map/all_gather | solution.py:58
  388.0 240.4 %reduce-scatter.2.cloned.1.call-start = ((), (), s32[]{:S(2)}) async-start(), calls=%async_computation.6 | async-start | bytes 4456448 | tf_op jit(solution)/shard_map/reduce_scatter | solution.py:66
  486.5 143.7 %copy-start.1 = (bf16[256,32,128]{2,1,0:T(8,128)(2,1)S(1)}, bf16[256,32,128]{2,1,0:T(8,128)(2,1)}, u32[]{:S(2)}) copy-start(bf16[256,32,128]{2,1,0:T(8,128)(2,1)} %param.7) | copy-start | bytes 6291460
  529.6 0.7 copy-start.4
  529.6 0.7 copy-start.6
  529.6 1.0 copy-start.3
  529.6 1.0 copy-start.5
Sparse Core Ops, SparseCore 0:
  9.4 83.4 all-gather.4
  180.7 150.5 all-gather.6
  347.4 16.2 all-gather.8
  388.1 52.2 all-gather.10
  529.7 98.6 reduce-scatter.1
